TPU v7x, 32 devices: a whole 2x2x4 slice. The times are simulated.
32 devices in a mesh: frame: 8 (over y, x, core), query: 4 (over z).
Axes of the slice: x: 2, y: 2, z: 4, core: 2. Of those that a mesh axis runs over, the one named last changes fastest.
Arguments:
- features: bfloat16 [8, 4096, 256], P('frame'), may hold values from -4.375 to 4.375
- kernel: float32 [3, 3], replicated, may hold values from 0.2 to 1
- cotangent: float32 [2, 8, 4096], P(None, 'frame', 'query'), may hold values from -6 to 6
- query_frame: int32 [4096], P('query'), may hold values from 0 to 7
- query_pixel: int32 [4096], P('query'), may hold values from 0 to 4095
Outputs:
- query_grad: float32 [4096, 256], P('query')
- feature_grad: float32 [8, 4096, 256], P('frame', 'query')
All inputs are finite; a program needn't handle non-finite values.
Results may differ from a plain program's by a relative error of at most 0.0029.
Values may be sent and summed in bfloat16 or wider, within the bound.
No kernel may reach another device: no remote copies, remote signals or barrier semaphores. Data moves between devices by JAX's collectives and lax.ppermute only.
A program may use at most 128 MiB of HBM per device.

v0:
```python
import jax
import jax.numpy as jnp
from jax import lax
from jax.sharding import PartitionSpec as P

W = 64


def shifted(values, offset, margin, length):
    padded = jnp.pad(values, ((0, 0), (margin, margin)))
    return lax.slice_in_dim(padded, margin + offset, margin + offset + length, axis=1)


def shards(features, kernel, cotangent, query_frame, query_pixel):
    t_dev, pixels, chan = features.shape
    height = pixels // W
    margin = W + 1
    frame_base = lax.axis_index("frame") * t_dev
    local_frame = query_frame - frame_base
    owned = (local_frame >= 0) & (local_frame < t_dev)
    flat_rows = jnp.clip(local_frame, 0, t_dev - 1) * pixels + query_pixel
    flat_maps = features.reshape(t_dev * pixels, chan)
    picked = jnp.where(owned[:, None], flat_maps[flat_rows], 0).astype(jnp.float32)
    qfeat = lax.psum(picked.astype(jnp.bfloat16), "frame")
    where_pix = lax.iota(jnp.int32, pixels)
    column = where_pix % W
    row_pos = (where_pix // W).astype(jnp.float32) - (height - 1) / 2.0
    col_pos = column.astype(jnp.float32) - (W - 1) / 2.0
    col_masks = {
        -1: (column >= 1)[None, :],
        0: (column >= 0)[None, :],
        1: (column <= W - 2)[None, :],
    }
    frame_map = features[0]
    cost = lax.dot_general(
        qfeat, frame_map, (((1,), (1,)), ((), ())), preferred_element_type=jnp.float32
    )
    logits = jnp.zeros_like(cost)
    for a in (-1, 0, 1):
        for b in (-1, 0, 1):
            moved = shifted(cost, a * W + b, margin, pixels)
            logits = logits + kernel[a + 1, b + 1] * jnp.where(col_masks[b], moved, 0.0)
    top = jnp.max(logits, axis=1, keepdims=True)
    expo = jnp.exp(logits - top)
    prob = expo / jnp.sum(expo, axis=1, keepdims=True)
    pull = cotangent[0, 0][:, None] * row_pos[None, :] + cotangent[1, 0][:, None] * col_pos[None, :]
    mean_pull = jnp.sum(prob * pull, axis=1, keepdims=True)
    dlogit = prob * (pull - mean_pull)
    dcost = jnp.zeros_like(dlogit)
    for a in (-1, 0, 1):
        for b in (-1, 0, 1):
            masked = jnp.where(col_masks[b], dlogit, 0.0)
            dcost = dcost + kernel[a + 1, b + 1] * shifted(masked, -(a * W + b), margin, pixels)
    dcost = dcost.astype(jnp.bfloat16)
    query_part = jnp.dot(dcost, frame_map, preferred_element_type=jnp.float32)
    frame_terms = [
        lax.dot_general(dcost, qfeat, (((0,), (0,)), ((), ())), preferred_element_type=jnp.float32)
    ]
    feature_term = jnp.stack(frame_terms)
    query_grad = lax.psum(query_part, "frame")
    placed = jnp.where(owned[:, None], query_grad, 0.0)
    feature_term = (
        feature_term.reshape(t_dev * pixels, chan)
        .at[flat_rows]
        .add(placed)
        .reshape(t_dev, pixels, chan)
    )
    feature_grad = lax.psum_scatter(feature_term, "query", scatter_dimension=1, tiled=True)
    return (query_grad, feature_grad)


def solution(mesh):
    placed = (P("frame", None, None), P(), P(None, "frame", "query"), P("query"), P("query"))
    return jax.shard_map(
        shards,
        mesh=mesh,
        in_specs=placed,
        out_specs=(P("query", None), P("frame", "query", None)),
        check_vma=False,
    )
```

profile of v0, /device:TPU:0, one launch (start us, length us, event | category | flops | bytes accessed | tf_op | source)
XLA Modules:
  0.0 449.0 jit_solution(2033591671652492786)
XLA Ops:
  7.2 0.0 copy-start
  7.2 0.0 all-reduce.7.cloned.1.call-start
  7.2 0.8 compare_and_fusion
  8.1 0.7 broadcast_clamp_fusion
  8.8 0.0 copy-done
  8.8 3.9 gather_fusion
  12.7 1.0 broadcast_select_fusion.3
  13.7 0.0 all-reduce.7.cloned.1.call-update
  13.8 0.0 all-reduce.9.cloned.1.call-start
  13.8 1.7 fusion.43
  15.5 0.7 fusion.42
  16.3 55.2 %all-reduce.7.cloned.1.call-done = bf16[1024,256]{1,0:T(8,128)(2,1)} async-done(((bf16[1024,256]{1,0:T(8,128)(2,1)}), bf16[1024,256]{1,0:T(8,128)(2,1)}) %all-reduce.7.cloned.1.call-update) | async-done | bytes 524304 | tf_op jit(solution)/shard_map/psum | solution.py:24
  71.4 9.1 %fusion.39 = f32[1024,4096]{1,0:T(8,128)} fusion(bf16[1024,256]{1,0:T(8,128)(2,1)} %all-reduce.7.cloned.1.call-done, bf16[1,4096,256]{2,1,0:T(8,128)(2,1)S(1)} %copy-done), kind=kOutput, calls=%fused_computation.66 | convolution fusion | flops 2147483648 | bytes 19398656 | tf_op jit(solution)/shard_map/dot_general | solution.py:35
  80.6 85.7 %fusion.41 = (f32[1024]{0:T(1024)S(1)}, f32[1024,4096]{1,0:T(8,128)}) fusion(f32[]{:T(128)} %bitcast.9, f32[]{:T(128)} %bitcast.8, f32[]{:T(128)} %bitcast.7, f32[]{:T(128)} %bitcast.6, f32[1024,4096]{1,0:T(8,128)} %fusion.39, f32[]{:T(128)} %bitcast.5, f32[]{:T(128)} %bitcast.4, pred[4096]{0:T(1024)(128)(4,1)S(1)} %get-tuple-element.21, f32[]{:T(128)} %bitcast.3, ...), kind=kLoop, calls=%fused_computation.68 | loop fusion | flops 113245184 | bytes 33570852 | tf_op jit(solution)/shard_map/reduce_max | solution.py:43
  166.2 8.1 %fusion.22 = f32[1024]{0:T(1024)S(1)} fusion(f32[1024,4096]{1,0:T(8,128)} %get-tuple-element.5, f32[1024]{0:T(1024)S(1)} %get-tuple-element.4), kind=kLoop, calls=%fused_computation.36 | loop fusion | flops 8387584 | bytes 16785408 | tf_op jit(solution)/shard_map/reduce_sum | solution.py:45
  174.3 8.8 %multiply_reduce_fusion = f32[1024]{0:T(1024)S(1)} fusion(f32[4096]{0:T(1024)S(1)} %get-tuple-element.24, f32[1024]{0:T(1024)S(1)} %bitcast.25, f32[4096]{0:T(1024)S(1)} %get-tuple-element.23, f32[1024]{0:T(1024)S(1)} %bitcast.23, f32[1024]{0:T(1024)S(1)} %fusion.22, f32[1024,4096]{1,0:T(8,128)} %get-tuple-element.5, f32[1024]{0:T(1024)S(1)} %get-tuple-element.4), kind=kLoop, calls=%fused_computation.20 | loop fusion | flops 29359104 | bytes 16830464 | tf_op jit(solution)/shard_map/reduce_sum | solution.py:47
  183.1 15.2 %broadcast_select_fusion.1 = (f32[1024,4096]{1,0:T(8,128)}, f32[1024,4096]{1,0:T(8,128)S(1)}) fusion(pred[4096]{0:T(1024)(128)(4,1)S(1)} %fusion.34, f32[1024]{0:T(1024)S(1)} %multiply_reduce_fusion, f32[4096]{0:T(1024)S(1)} %get-tuple-element.24, f32[1024]{0:T(1024)S(1)} %bitcast.26, f32[4096]{0:T(1024)S(1)} %get-tuple-element.23, f32[1024]{0:T(1024)S(1)} %bitcast.24, ...), kind=kLoop, calls=%fused_computation.38 | loop fusion | flops 33554432 | bytes 50388992 | tf_op jit(solution)/shard_map/jit(_where)/select_n | solution.py:52
  198.3 11.7 %broadcast_select_fusion = (f32[1024,4096]{1,0:T(8,128)}, f32[1024,4096]{1,0:T(8,128)}) fusion(f32[1024,4096]{1,0:T(8,128)S(1)} %get-tuple-element.3, pred[4096]{0:T(1024)(128)(4,1)S(1)} %get-tuple-element.21, pred[4096]{0:T(1024)(128)(4,1)S(1)} %get-tuple-element.22), kind=kLoop, calls=%fused_computation.37 | loop fusion | flops 8388608 | bytes 50339840 | tf_op jit(solution)/shard_map/jit(_where)/select_n | solution.py:52
  210.0 0.0 copy-start.2
  210.0 79.9 %fusion.9 = bf16[1024,4096]{1,0:T(8,128)(2,1)S(1)} fusion(f32[1024,4096]{1,0:T(8,128)} %get-tuple-element.9, f32[1024,4096]{1,0:T(8,128)} %get-tuple-element.8, f32[1024,4096]{1,0:T(8,128)} %get-tuple-element.2, f32[]{:T(128)} %bitcast.9, f32[]{:T(128)} %bitcast.8, f32[]{:T(128)} %bitcast.7, f32[]{:T(128)} %bitcast.6, f32[]{:T(128)} %bitcast.5, f32[]{:T(128)} %bitcast.4, ...), kind=kLoop, calls=%fused_computation.13 | loop fusion | flops 75497472 | bytes 58720292 | tf_op jit(solution)/shard_map/convert_element_type | solution.py:54
  290.0 0.0 copy-start.1
  290.0 3.2 copy-done.1
  293.2 3.3 fusion.37
  296.5 0.0 all-reduce.9.cloned.1.call-update
  296.5 0.0 reduce-scatter.2.cloned.1.call-start
  296.6 0.0 copy-done.2
  296.6 7.8 %fusion.44 = f32[4096,256]{1,0:T(8,128)} fusion(bf16[1024,4096]{1,0:T(8,128)(2,1)} %copy-done.1, bf16[1024,256]{1,0:T(8,128)(2,1)S(1)} %copy-done.2), kind=kOutput, calls=%fused_computation.71 | convolution fusion | flops 2147483648 | bytes 13107200 | tf_op jit(solution)/shard_map/dot_general | solution.py:57
  304.4 48.3 %all-reduce.9.cloned.1.call-done = f32[1024,256]{1,0:T(8,128)} async-done(((f32[1024,256]{1,0:T(8,128)}), f32[1024,256]{1,0:T(8,128)}) %all-reduce.9.cloned.1.call-update) | async-done | bytes 1048592 | tf_op jit(solution)/shard_map/psum | solution.py:60
  352.7 11.2 %scatter_custom_fusion = f32[4096,256]{1,0:T(8,128)} fusion(f32[4096,256]{1,0:T(8,128)} %fusion.44, s32[1024]{0:T(1024)S(1)} %get-tuple-element.7, f32[1024,256]{1,0:T(8,128)} %all-reduce.9.cloned.1.call-done, f32[]{:T(128)} %constant.51.clone.1, pred[1024]{0:T(1024)(128)(4,1)S(1)} %compare_and_fusion), kind=kCustom, calls=%fused_computation.40 | custom fusion | flops 524288 | bytes 5244416 | tf_op jit(solution)/shard_map/scatter-add | solution.py:65
  363.9 0.0 reduce-scatter.2.cloned.1.call-update
  364.0 76.2 %reduce-scatter.2.cloned.1.call-done = f32[1,1024,256]{2,1,0:T(8,128)} async-done(((f32[1,4096,256]{2,1,0:T(8,128)}), f32[1,1024,256]{2,1,0:T(8,128)}) %reduce-scatter.2.cloned.1.call-update) | async-done | bytes 1048592 | tf_op jit(solution)/shard_map/reduce_scatter | solution.py:68
  440.2 2.3 copy.10
  (3 shorter events, 0.0 us)
Async XLA Ops:
  7.2 1.6 copy-start
  7.2 64.2 %all-reduce.7.cloned.1.call-start = ((), (), s32[]{:S(2)}) async-start(), calls=%async_computation.1 | async-start | bytes 1048576 | tf_op jit(solution)/shard_map/psum | solution.py:24
  13.8 338.9 %all-reduce.9.cloned.1.call-start = ((), (), s32[]{:S(2)}) async-start(), calls=%async_computation.2 | async-start | bytes 2097152 | tf_op jit(solution)/shard_map/psum | solution.py:60
  210.0 86.6 %copy-start.2 = (bf16[1024,256]{1,0:T(8,128)(2,1)S(1)}, bf16[1024,256]{1,0:T(8,128)(2,1)}, u32[]{:S(2)}) copy-start(bf16[1024,256]{1,0:T(8,128)(2,1)} %all-reduce.7.cloned.1.call-done) | copy-start | bytes 1572868
  290.0 3.2 copy-start.1
  296.5 143.6 %reduce-scatter.2.cloned.1.call-start = ((), (), s32[]{:S(2)}) async-start(), calls=%async_computation.3 | async-start | bytes 5242880 | tf_op jit(solution)/shard_map/reduce_scatter | solution.py:68
Sparse Core Ops, SparseCore 0:
  13.9 57.4 all-reduce.6
  296.7 55.9 all-reduce.8
  364.1 76.0 reduce-scatter.1
where the time goes:
time: 450 us; the launch traced here: 449 us
  other arithmetic  223 us (50%)
  waiting for transfers between devices  180 us (40%)
  matrix products  20.3 us (5%)
  between operations  13.8 us (3%)
  local copies, waits for them, and re-layouts  11.8 us (3%)
    reduce_max x1, other arithmetic, shards(): top = jnp.max(logits, axis=1, keepdims=True)  85.7 us
    convert_element_type x1, other arithmetic, shards(): dcost = dcost.astype(jnp.bfloat16)  79.9 us
    reduce_scatter x1, waiting for transfers between devices, shards(): lax.psum_scatter(feature_term, 'query', scatter_dimension=1, tiled=True)  76.2 us
    psum x1, waiting for transfers between devices, shards(): qfeat = lax.psum(picked.astype(jnp.bfloat16), 'frame')  55.2 us
    psum x1, waiting for transfers between devices, shards(): query_grad = lax.psum(query_part, 'frame')  48.3 us
    select_n x2, other arithmetic, shards(): masked = jnp.where(col_masks[b], dlogit, 0.0)  26.9 us
    scatter-add x1, other arithmetic, shards(): feature_term = feature_term.reshape(t_dev * pixels, chan).at[flat_rows].a...  11.2 us
    dot_general x1, matrix products, shards(): lax.dot_general(qfeat, frame_map, (((1,), (1,)), ((), ())), preferred_ele...  9.14 us
  transfers between devices with their start and end apart: 3, of which 3 were waited for; matrix products, arithmetic and copies ran while one was open for 2% of the time, Pallas kernels for 0%

commit v1 on v0

--- a/solution.py
+++ b/solution.py
@@ -21,7 +21,9 @@
     flat_rows = jnp.clip(local_frame, 0, t_dev - 1) * pixels + query_pixel
     flat_maps = features.reshape(t_dev * pixels, chan)
     picked = jnp.where(owned[:, None], flat_maps[flat_rows], 0).astype(jnp.float32)
-    qfeat = lax.psum(picked.astype(jnp.bfloat16), "frame")
+    own = picked.astype(jnp.bfloat16)
+    shards_2 = lax.all_gather(own, "frame", axis=0, tiled=False)
+    qfeat = shards_2.sum(axis=0)
     where_pix = lax.iota(jnp.int32, pixels)
     column = where_pix % W
     row_pos = (where_pix // W).astype(jnp.float32) - (height - 1) / 2.0

time: 450 us -> 434 us (0.964)
  waiting for transfers between devices: 180 us -> 162 us
    psum x1 -> x0, waiting for transfers between devices: 55.2 us -> none  [shards(): qfeat = lax.psum(picked.astype(jnp.bfloat16), 'frame')]
    all_gather x0 -> x1, waiting for transfers between devices: none -> 37 us  [shards(): shards_2 = lax.all_gather(own, 'frame', axis=0, tiled=False)]
where the time goes in v1:
time: 434 us; the launch traced here: 433 us
  other arithmetic  226 us (52%)
  waiting for transfers between devices  162 us (37%)
  matrix products  19.2 us (4%)
  between operations  13.8 us (3%)
  local copies, waits for them, and re-layouts  11.8 us (3%)
    reduce_max x1, other arithmetic, shards(): top = jnp.max(logits, axis=1, keepdims=True)  85.4 us
    convert_element_type x1, other arithmetic, shards(): dcost = dcost.astype(jnp.bfloat16)  79.6 us
    reduce_scatter x1, waiting for transfers between devices, shards(): lax.psum_scatter(feature_term, 'query', scatter_dimension=1, tiled=True)  76.2 us
    psum x1, waiting for transfers between devices, shards(): query_grad = lax.psum(query_part, 'frame')  49 us
    all_gather x1, waiting for transfers between devices, shards(): shards_2 = lax.all_gather(own, 'frame', axis=0, tiled=False)  37 us
    select_n x2, other arithmetic, shards(): masked = jnp.where(col_masks[b], dlogit, 0.0)  26.9 us
    scatter-add x1, other arithmetic, shards(): feature_term = feature_term.reshape(t_dev * pixels, chan).at[flat_rows].a...  11.2 us
    reduce_sum x1, other arithmetic, shards(): mean_pull = jnp.sum(prob * pull, axis=1, keepdims=True)  8.81 us
  transfers between devices with their start and end apart: 3, of which 3 were waited for; matrix products, arithmetic and copies ran while one was open for 2% of the time, Pallas kernels for 0%

profile of v1, /device:TPU:0, one launch (start us, length us, event | category | flops | bytes accessed | tf_op | source)
XLA Modules:
  0.0 432.9 jit_solution(9875729662502992714)
XLA Ops:
  7.2 0.0 copy-start
  7.2 0.0 all-gather.2.cloned.1.call-start
  7.2 0.8 compare_and_fusion
  8.1 0.7 broadcast_clamp_fusion
  8.8 0.0 copy-done
  8.8 3.9 gather_fusion
  12.7 1.0 bitcast_select_fusion
  13.7 0.0 all-gather.2.cloned.1.call-update
  13.8 0.0 all-reduce.6.cloned.1.call-start
  13.8 1.7 fusion.43
  15.5 0.7 fusion.42
  16.2 37.0 %all-gather.2.cloned.1.call-done = bf16[8,1024,256]{2,1,0:T(8,128)(2,1)} async-done(((bf16[1,1024,256]{2,1,0:T(8,128)(2,1)}), bf16[8,1024,256]{2,1,0:T(8,128)(2,1)}) %all-gather.2.cloned.1.call-update) | async-done | bytes 4194320 | tf_op jit(solution)/shard_map/all_gather | solution.py:25
  53.2 3.0 reduce_sum.30
  56.3 8.1 %fusion.39 = f32[1024,4096]{1,0:T(8,128)} fusion(bf16[1024,256]{1,0:T(8,128)(2,1)S(1)} %reduce_sum.30, bf16[1,4096,256]{2,1,0:T(8,128)(2,1)S(1)} %copy-done), kind=kOutput, calls=%fused_computation.66 | convolution fusion | flops 2147483648 | bytes 19398656 | tf_op jit(solution)/shard_map/dot_general | solution.py:37
  64.4 85.4 %fusion.41 = (f32[1024]{0:T(1024)S(1)}, f32[1024,4096]{1,0:T(8,128)}) fusion(f32[]{:T(128)} %bitcast.10, f32[]{:T(128)} %bitcast.9, f32[]{:T(128)} %bitcast.8, f32[]{:T(128)} %bitcast.7, f32[1024,4096]{1,0:T(8,128)} %fusion.39, f32[]{:T(128)} %bitcast.6, f32[]{:T(128)} %bitcast.5, pred[4096]{0:T(1024)(128)(4,1)S(1)} %get-tuple-element.21, f32[]{:T(128)} %bitcast.4, ...), kind=kLoop, calls=%fused_computation.68 | loop fusion | flops 113245184 | bytes 33570852 | tf_op jit(solution)/shard_map/reduce_max | solution.py:45
  149.8 8.1 %fusion.22 = f32[1024]{0:T(1024)S(1)} fusion(f32[1024,4096]{1,0:T(8,128)} %get-tuple-element.5, f32[1024]{0:T(1024)S(1)} %get-tuple-element.4), kind=kLoop, calls=%fused_computation.36 | loop fusion | flops 8387584 | bytes 16785408 | tf_op jit(solution)/shard_map/reduce_sum | solution.py:47
  157.9 8.8 %multiply_reduce_fusion = f32[1024]{0:T(1024)S(1)} fusion(f32[4096]{0:T(1024)S(1)} %get-tuple-element.24, f32[1024]{0:T(1024)S(1)} %bitcast.27, f32[4096]{0:T(1024)S(1)} %get-tuple-element.23, f32[1024]{0:T(1024)S(1)} %bitcast.25, f32[1024]{0:T(1024)S(1)} %fusion.22, f32[1024,4096]{1,0:T(8,128)} %get-tuple-element.5, f32[1024]{0:T(1024)S(1)} %get-tuple-element.4), kind=kLoop, calls=%fused_computation.20 | loop fusion | flops 29359104 | bytes 16830464 | tf_op jit(solution)/shard_map/reduce_sum | solution.py:49
  166.7 15.2 %broadcast_select_fusion.1 = (f32[1024,4096]{1,0:T(8,128)}, f32[1024,4096]{1,0:T(8,128)S(1)}) fusion(pred[4096]{0:T(1024)(128)(4,1)S(1)} %fusion.34, f32[1024]{0:T(1024)S(1)} %multiply_reduce_fusion, f32[4096]{0:T(1024)S(1)} %get-tuple-element.24, f32[1024]{0:T(1024)S(1)} %bitcast.28, f32[4096]{0:T(1024)S(1)} %get-tuple-element.23, f32[1024]{0:T(1024)S(1)} %bitcast.26, ...), kind=kLoop, calls=%fused_computation.38 | loop fusion | flops 33554432 | bytes 50388992 | tf_op jit(solution)/shard_map/jit(_where)/select_n | solution.py:54
  181.9 11.7 %broadcast_select_fusion = (f32[1024,4096]{1,0:T(8,128)}, f32[1024,4096]{1,0:T(8,128)}) fusion(f32[1024,4096]{1,0:T(8,128)S(1)} %get-tuple-element.3, pred[4096]{0:T(1024)(128)(4,1)S(1)} %get-tuple-element.21, pred[4096]{0:T(1024)(128)(4,1)S(1)} %get-tuple-element.22), kind=kLoop, calls=%fused_computation.37 | loop fusion | flops 8388608 | bytes 50339840 | tf_op jit(solution)/shard_map/jit(_where)/select_n | solution.py:54
  193.6 79.6 %fusion.9 = bf16[1024,4096]{1,0:T(8,128)(2,1)S(1)} fusion(f32[1024,4096]{1,0:T(8,128)} %get-tuple-element.9, f32[1024,4096]{1,0:T(8,128)} %get-tuple-element.8, f32[1024,4096]{1,0:T(8,128)} %get-tuple-element.2, f32[]{:T(128)} %bitcast.10, f32[]{:T(128)} %bitcast.9, f32[]{:T(128)} %bitcast.8, f32[]{:T(128)} %bitcast.7, f32[]{:T(128)} %bitcast.6, f32[]{:T(128)} %bitcast.5, ...), kind=kLoop, calls=%fused_computation.13 | loop fusion | flops 75497472 | bytes 58720292 | tf_op jit(solution)/shard_map/convert_element_type | solution.py:56
  273.3 0.0 copy-start.1
  273.3 3.2 copy-done.1
  276.5 3.3 fusion.37
  279.8 0.0 all-reduce.6.cloned.1.call-update
  279.8 0.0 reduce-scatter.2.cloned.1.call-start
  279.9 7.8 %fusion.44 = f32[4096,256]{1,0:T(8,128)} fusion(bf16[1024,4096]{1,0:T(8,128)(2,1)} %copy-done.1, bf16[1024,256]{1,0:T(8,128)(2,1)S(1)} %reduce_sum.30), kind=kOutput, calls=%fused_computation.71 | convolution fusion | flops 2147483648 | bytes 13107200 | tf_op jit(solution)/shard_map/dot_general | solution.py:59
  287.7 49.0 %all-reduce.6.cloned.1.call-done = f32[1024,256]{1,0:T(8,128)} async-done(((f32[1024,256]{1,0:T(8,128)}), f32[1024,256]{1,0:T(8,128)}) %all-reduce.6.cloned.1.call-update) | async-done | bytes 1048592 | tf_op jit(solution)/shard_map/psum | solution.py:62
  336.7 11.2 %scatter_custom_fusion = f32[4096,256]{1,0:T(8,128)} fusion(f32[4096,256]{1,0:T(8,128)} %fusion.44, s32[1024]{0:T(1024)S(1)} %get-tuple-element.7, f32[1024,256]{1,0:T(8,128)} %all-reduce.6.cloned.1.call-done, f32[]{:T(128)} %constant.52.clone.1, pred[1024]{0:T(1024)(128)(4,1)S(1)} %compare_and_fusion), kind=kCustom, calls=%fused_computation.40 | custom fusion | flops 524288 | bytes 5244416 | tf_op jit(solution)/shard_map/scatter-add | solution.py:67
  347.9 0.0 reduce-scatter.2.cloned.1.call-update
  347.9 76.2 %reduce-scatter.2.cloned.1.call-done = f32[1,1024,256]{2,1,0:T(8,128)} async-done(((f32[1,4096,256]{2,1,0:T(8,128)}), f32[1,1024,256]{2,1,0:T(8,128)}) %reduce-scatter.2.cloned.1.call-update) | async-done | bytes 1048592 | tf_op jit(solution)/shard_map/reduce_scatter | solution.py:70
  424.1 2.3 copy.9
  (3 shorter events, 0.0 us)
Async XLA Ops:
  7.2 1.6 copy-start
  7.2 46.0 %all-gather.2.cloned.1.call-start = ((), (), s32[]{:S(2)}) async-start(), calls=%async_computation.1 | async-start | bytes 4718592 | tf_op jit(solution)/shard_map/all_gather | solution.py:25
  13.8 322.9 %all-reduce.6.cloned.1.call-start = ((), (), s32[]{:S(2)}) async-start(), calls=%async_computation.2 | async-start | bytes 2097152 | tf_op jit(solution)/shard_map/psum | solution.py:62
  273.3 3.2 copy-start.1
  279.8 144.3 %reduce-scatter.2.cloned.1.call-start = ((), (), s32[]{:S(2)}) async-start(), calls=%async_computation.3 | async-start | bytes 5242880 | tf_op jit(solution)/shard_map/reduce_scatter | solution.py:70
Sparse Core Ops, SparseCore 0:
  13.9 39.2 all-gather.1
  279.9 56.6 all-reduce.5
  348.0 76.0 reduce-scatter.1
